TPU v7x, 256 devices: a whole 4x4x8 slice. The times are simulated.
256 devices in a mesh: ctx: 32 (over x, y, core), head: 8 (over z).
Axes of the slice: x: 4, y: 4, z: 8, core: 2. Of those that a mesh axis runs over, the one named last changes fastest.
Arguments:
- lin_q: bfloat16 [4096, 8192], P('ctx', 'head'), may hold values from -5 to 5
- lin_k: bfloat16 [4096, 8192], P('ctx', 'head'), may hold values from -5 to 5
- lin_v: bfloat16 [4096, 8192], P('ctx', 'head'), may hold values from -52 to 52
- log_decay: float32 [4096, 64], P('ctx', 'head'), may hold values from -1.5 to 0
- norm_gain: float32 [8192], P('head'), may hold values from 0.25 to 1.75
- lin_cot: bfloat16 [4096, 8192], P('ctx', 'head'), may hold values from -5 to 5
- soft_q: bfloat16 [4096, 8192], P('ctx', 'head'), may hold values from -5 to 5
- soft_k: bfloat16 [4096, 1024], P('ctx', 'head'), may hold values from -5 to 5
- soft_v: bfloat16 [4096, 1024], P('ctx', 'head'), may hold values from -5 to 5
- soft_cot: bfloat16 [4096, 8192], P('ctx', 'head'), may hold values from -5 to 5
Outputs:
- lin_dq: float32 [4096, 8192], P('ctx', 'head')
- lin_dk: float32 [4096, 8192], P('ctx', 'head')
- lin_dv: float32 [4096, 8192], P('ctx', 'head')
- gain_grad: float32 [8192], P('head')
- soft_dq: float32 [4096, 8192], P('ctx', 'head')
- soft_dk: float32 [4096, 1024], P('ctx', 'head')
- soft_dv: float32 [4096, 1024], P('ctx', 'head')
All inputs are finite; a program needn't handle non-finite values.
Results may differ from a plain program's by a relative error of at most 0.018.
Values may be sent and summed in bfloat16 or wider, within the bound.
A program may use at most 128 MiB of HBM per device.

v0:
```python
import math

import jax
import jax.numpy as jnp
from jax import lax
from jax.sharding import PartitionSpec as P

HEAD_DIM = 128
LINEAR_HEADS = 64
GROUP = 8


EPS = 1e-06
NEG = -1e30


def entering_2(value, axis, join, neutral):
    count, mine = (lax.axis_size(axis), lax.axis_index(axis))
    pieces = jax.tree.map(lambda part: lax.all_gather(part, axis), value)
    running = jax.tree.map(
        lambda part, zero: jnp.full_like(part, 0) + jnp.asarray(zero, part.dtype), value, neutral
    )

    def lap(position, running):
        longer = join(running, jax.tree.map(lambda part: part[position], pieces))
        return jax.tree.map(lambda new, old: jnp.where(position < mine, new, old), longer, running)

    return lax.fori_loop(0, count - 1, lap, running)


def entering_3(shard, axis, join, neutral):
    count = lax.axis_size(axis)
    place = lax.axis_index(axis)
    ahead = count - 1 - place
    gathered = jax.tree.map(
        lambda a, kind: lax.all_gather(a.astype(kind), axis), shard, (jnp.bfloat16, jnp.bfloat16)
    )
    state = jax.tree.map(lambda a, e: jnp.zeros_like(a) + jnp.asarray(e, a.dtype), shard, neutral)

    def one(lap, state):
        source = count - 1 - lap
        return join(
            state,
            jax.tree.map(
                lambda a, own: lax.dynamic_index_in_dim(a, source, 0, False).astype(own.dtype),
                gathered,
                shard,
            ),
        )

    return lax.fori_loop(0, ahead, one, state)


def lightning_part(lin_q, lin_k, lin_v, log_decay, norm_gain, lin_cot):
    local_rows = lin_q.shape[0]
    head_count = log_decay.shape[1]
    score_scale = HEAD_DIM ** (-0.5)
    feat_width = LINEAR_HEADS * HEAD_DIM
    shape_three = (local_rows, head_count, HEAD_DIM)
    queries = lin_q.reshape(shape_three)
    key_rows = lin_k.reshape(shape_three)
    values = lin_v.reshape(shape_three)
    log_cum = jnp.cumsum(log_decay, axis=0)
    decay_total = log_cum[-1]
    key_decay = jnp.exp(decay_total[None, :] - log_cum)
    query_decay = jnp.exp(log_cum)
    keys_dec = (key_rows * key_decay[:, :, None]).astype(jnp.bfloat16)
    local_state = jnp.einsum("thd,the->hde", keys_dec, values, preferred_element_type=jnp.float32)
    zero_state = jnp.zeros_like(local_state)
    zero_total = jnp.zeros_like(decay_total)

    def chain_forward(earlier, later):
        return (earlier[0] + later[0], jnp.exp(later[0])[:, None, None] * earlier[1] + later[1])

    _, entering = entering_2(
        (decay_total, local_state), "ctx", chain_forward, (zero_total, zero_state)
    )
    entering = entering.astype(jnp.bfloat16)
    offsets = jnp.arange(local_rows, dtype=jnp.int32)
    causal = offsets[None, :] <= offsets[:, None]
    log_gap = log_cum[:, None, :] - log_cum[None, :, :]
    decay_mat = jnp.transpose(
        jnp.where(causal[:, :, None], jnp.exp(jnp.minimum(log_gap, 0.0)), 0.0), (2, 0, 1)
    )
    weights = (
        jnp.einsum("thd,shd->hts", queries, key_rows, preferred_element_type=jnp.float32)
        * score_scale
        * decay_mat
    ).astype(jnp.bfloat16)
    output = jnp.einsum(
        "hts,she->the", weights, values, preferred_element_type=jnp.float32
    ) + score_scale * query_decay[:, :, None] * jnp.einsum(
        "thd,hde->the", queries, entering, preferred_element_type=jnp.float32
    )
    flat_out = output.reshape(local_rows, head_count * HEAD_DIM)
    scaled_cot = lin_cot * norm_gain[None, :]
    square_sum = lax.psum(jnp.sum(flat_out * flat_out, axis=1), "head")
    inv_rms = lax.rsqrt(square_sum / feat_width + EPS)
    normed = flat_out * inv_rms[:, None]
    mean_cross = lax.psum(jnp.sum(scaled_cot * normed, axis=1), "head") / feat_width
    out_cot = ((scaled_cot - normed * mean_cross[:, None]) * inv_rms[:, None]).astype(jnp.bfloat16)
    gain_grad = lax.psum(jnp.sum(lin_cot * normed, axis=0), "ctx")
    out_cot = out_cot.reshape(shape_three)
    queries_dec = (queries * query_decay[:, :, None]).astype(jnp.bfloat16)
    local_grad = jnp.einsum(
        "thd,the->hde", queries_dec, out_cot, preferred_element_type=jnp.float32
    )

    def chain_backward(earlier, later):
        return (earlier[0] + later[0], later[1] + jnp.exp(later[0])[:, None, None] * earlier[1])

    _, after = entering_3(
        (decay_total, local_grad), "ctx", chain_backward, (zero_total, zero_state)
    )
    after = after.astype(jnp.bfloat16)
    dweights = (
        jnp.einsum("the,she->hts", out_cot, values, preferred_element_type=jnp.float32)
        * score_scale
        * decay_mat
    ).astype(jnp.bfloat16)
    grad_q = jnp.einsum(
        "hts,shd->thd", dweights, key_rows, preferred_element_type=jnp.float32
    ) + score_scale * query_decay[:, :, None] * jnp.einsum(
        "the,hde->thd", out_cot, entering, preferred_element_type=jnp.float32
    )
    grad_k = jnp.einsum(
        "hts,thd->shd", dweights, queries, preferred_element_type=jnp.float32
    ) + score_scale * key_decay[:, :, None] * jnp.einsum(
        "she,hde->shd", values, after, preferred_element_type=jnp.float32
    )
    grad_v = jnp.einsum(
        "hts,the->she", weights, out_cot, preferred_element_type=jnp.float32
    ) + score_scale * key_decay[:, :, None] * jnp.einsum(
        "shd,hde->she", key_rows, after, preferred_element_type=jnp.float32
    )
    flat_shape = (local_rows, head_count * HEAD_DIM)
    return (
        grad_q.reshape(flat_shape),
        grad_k.reshape(flat_shape),
        grad_v.reshape(flat_shape),
        gain_grad,
    )


def softmax_part(soft_q, soft_k, soft_v, soft_cot):
    local_rows = soft_q.shape[0]
    kv_count = soft_k.shape[1] // HEAD_DIM
    key_width = kv_count * HEAD_DIM
    score_scale = HEAD_DIM ** (-0.5)
    queries = soft_q.reshape(local_rows, kv_count, GROUP, HEAD_DIM)
    cot_rows = soft_cot.reshape(local_rows, kv_count, GROUP, HEAD_DIM)
    stacked = jnp.concatenate([soft_k, soft_v], axis=1)
    ctx_count = lax.axis_size("ctx")
    seq_total = local_rows * ctx_count
    my_index = lax.axis_index("ctx")
    query_first = my_index * local_rows
    query_pos = query_first + jnp.arange(local_rows, dtype=jnp.int32)

    def block_scores(key_block, block_first):
        key_count = key_block.shape[0]
        key_part = key_block[:, :key_width].reshape(key_count, kv_count, HEAD_DIM)
        value_part = key_block[:, key_width:].reshape(key_count, kv_count, HEAD_DIM)
        scores = (
            jnp.einsum("tkgd,nkd->kgtn", queries, key_part, preferred_element_type=jnp.float32)
            * score_scale
        )
        allowed = (block_first + jnp.arange(key_count, dtype=jnp.int32))[None, :] <= query_pos[
            :, None
        ]
        return (key_part, value_part, scores, allowed)

    def over_blocks(step_fn, running, shard_rows):
        total_rows = shard_rows.shape[0]
        block_rows = math.gcd(total_rows, 512)
        grouped = shard_rows.reshape(total_rows // block_rows, block_rows, shard_rows.shape[1])

        def visit(partial_state, scan_item):
            block_index, key_block = scan_item
            block_first = block_index * block_rows
            needed = block_first <= query_first + local_rows - 1
            return (
                lax.cond(
                    needed,
                    lambda inner: step_fn(inner, key_block, block_first),
                    lambda inner: inner,
                    partial_state,
                ),
                None,
            )

        running, _ = lax.scan(
            visit, running, (jnp.arange(grouped.shape[0], dtype=jnp.int32), grouped)
        )
        return running

    def stat_step(running, key_block, block_first):
        run_max, run_sum, run_acc = running
        _, value_part, scores, allowed = block_scores(key_block, block_first)
        block_max = jnp.max(jnp.where(allowed, scores, NEG), axis=-1)
        new_max = jnp.maximum(run_max, block_max)
        probs = jnp.exp(jnp.where(allowed, scores - new_max[..., None], NEG))
        factor = jnp.exp(run_max - new_max)
        run_sum = run_sum * factor + jnp.sum(probs, axis=-1)
        probs_high = probs.astype(jnp.bfloat16)
        probs_low = (probs - probs_high.astype(jnp.float32)).astype(jnp.bfloat16)
        weighted = jnp.einsum(
            "kgtn,nkd->kgtd", probs_high, value_part, preferred_element_type=jnp.float32
        ) + jnp.einsum("kgtn,nkd->kgtd", probs_low, value_part, preferred_element_type=jnp.float32)
        run_acc = run_acc * factor[..., None] + weighted
        return (new_max, run_sum, run_acc)

    stat_init = (
        jnp.full((kv_count, GROUP, local_rows), NEG, jnp.float32),
        jnp.zeros((kv_count, GROUP, local_rows), jnp.float32),
        jnp.zeros((kv_count, GROUP, local_rows, HEAD_DIM), jnp.float32),
    )
    run_max, run_sum, run_acc = over_blocks(
        stat_step, stat_init, lax.all_gather(stacked, "ctx", axis=0, tiled=True)
    )
    log_sum = run_max + jnp.log(run_sum)
    attn_out = run_acc / run_sum[..., None]
    delta = jnp.sum(jnp.transpose(cot_rows, (1, 2, 0, 3)) * attn_out, axis=-1)

    def grad_terms(key_block, block_first):
        key_part, value_part, scores, allowed = block_scores(key_block, block_first)
        key_count = key_block.shape[0]
        probs = jnp.exp(jnp.where(allowed, scores - log_sum[..., None], NEG))
        dprobs = jnp.einsum(
            "tkgd,nkd->kgtn", cot_rows, value_part, preferred_element_type=jnp.float32
        )
        dscores = (probs * (dprobs - delta[..., None]) * score_scale).astype(jnp.bfloat16)
        q_term = jnp.einsum("kgtn,nkd->kgtd", dscores, key_part, preferred_element_type=jnp.float32)
        key_new = jnp.einsum("kgtn,tkgd->nkd", dscores, queries, preferred_element_type=jnp.float32)
        value_new = jnp.einsum(
            "kgtn,tkgd->nkd",
            probs.astype(jnp.bfloat16),
            cot_rows,
            preferred_element_type=jnp.float32,
        )
        fresh = jnp.concatenate(
            [key_new.reshape(key_count, key_width), value_new.reshape(key_count, key_width)], axis=1
        )
        return (q_term, fresh)

    def grad_step(running, key_block, block_first):
        q_grad, key_buffer = running
        q_term, fresh = grad_terms(key_block, block_first)
        current = lax.dynamic_slice_in_dim(key_buffer, block_first, key_block.shape[0], 0)
        key_buffer = lax.dynamic_update_slice_in_dim(key_buffer, current + fresh, block_first, 0)
        return (q_grad + q_term, key_buffer)

    zero_grad = jnp.zeros((kv_count, GROUP, local_rows, HEAD_DIM), jnp.float32)
    grad_init = (zero_grad, jnp.zeros((seq_total, 2 * key_width), jnp.float32))
    q_grad, key_buffer = over_blocks(
        grad_step, grad_init, lax.all_gather(stacked, "ctx", axis=0, tiled=True)
    )
    key_sums = lax.psum_scatter(
        key_buffer.astype(jnp.bfloat16), "ctx", scatter_dimension=0, tiled=True
    ).astype(jnp.float32)
    soft_dq = jnp.transpose(q_grad, (2, 0, 1, 3)).reshape(local_rows, kv_count * GROUP * HEAD_DIM)
    return (soft_dq, key_sums[:, :key_width], key_sums[:, key_width:])


def on_device(lin_q, lin_k, lin_v, log_decay, norm_gain, lin_cot, soft_q, soft_k, soft_v, soft_cot):
    lin_dq, lin_dk, lin_dv, gain_grad = lightning_part(
        lin_q, lin_k, lin_v, log_decay, norm_gain, lin_cot
    )
    soft_dq, soft_dk, soft_dv = softmax_part(soft_q, soft_k, soft_v, soft_cot)
    return (lin_dq, lin_dk, lin_dv, gain_grad, soft_dq, soft_dk, soft_dv)


def solution(mesh):
    return jax.shard_map(
        on_device,
        mesh=mesh,
        in_specs=(
            P("ctx", "head"),
            P("ctx", "head"),
            P("ctx", "head"),
            P("ctx", "head"),
            P("head"),
            P("ctx", "head"),
            P("ctx", "head"),
            P("ctx", "head"),
            P("ctx", "head"),
            P("ctx", "head"),
        ),
        out_specs=(
            P("ctx", "head"),
            P("ctx", "head"),
            P("ctx", "head"),
            P("head"),
            P("ctx", "head"),
            P("ctx", "head"),
            P("ctx", "head"),
        ),
        check_vma=False,
    )
```

profile of v0, /device:TPU:32, one launch (start us, length us, event | category | flops | bytes accessed | tf_op | source)
XLA Modules:
  0.0 477.4 jit_solution(7162641735852269572)
XLA Ops:
  7.2 1.5 pad_maximum_fusion
  15.5 23.6 %all-gather.2 = f32[32,1,8]{2,1,0:T(1,128)} all-gather(f32[1,1,8]{2,1,0:T(1,128)S(1)} %get-tuple-element.755), channel_id=1, replica_groups=mesh['ctx'=32,'head'=8] {'ctx'}, dimensions={0}, use_global_device_ids=true | all-gather | bytes 1056 | tf_op jit(solution)/shard_map/all_gather | solution.py:19
  40.2 22.1 %all-gather.8.cloned.1.call-done = bf16[4096,256]{1,0:T(8,128)(2,1)} async-done(((bf16[128,256]{1,0:T(8,128)(2,1)}), bf16[4096,256]{1,0:T(8,128)(2,1)}) %all-gather.8.cloned.1.call-update) | async-done | bytes 2097168 | tf_op jit(solution)/shard_map/all_gather | solution.py:255
  62.4 14.0 %while.61 = (s32[]{:T(128)}, f32[1,8,128]{2,1,0:T(8,128)S(1)}, f32[1,8,128]{2,1,0:T(8,128)S(1)}, f32[1,8,128,128]{3,2,1,0:T(8,128)S(1)}, s32[8]{0:T(128)S(1)}, /...) while((s32[]{:T(128)}, f32[1,8,128]{2,1,0:T(8,128)S(1)}, ...), condition=%wide.region_16.17_spmd.clone, body=%wide.region_11.16_spmd.clone.sunk | while | flops 412552832 | bytes 12069151 | solution.py:191
  63.7 3.6 conditional.6
  78.8 2.4 broadcast_in_dim.46
  82.1 30.0 %while.62 = (s32[]{:T(128)}, f32[1,8,128,128]{3,2,1,0:T(8,128)}, f32[4096,256]{0,1:T(8,128)}, s32[8]{0:T(128)}, s32[]{:T(128)}, /*index=5*/bf16[8,512,256]{2,1,0...) while((s32[]{:T(128)}, f32[1,8,128,128]{3,2,1,0:T(8,128)}, ...), condition=%wide.region_21.22_spmd.clone, body=%wide.region_18.21_spmd.clone.sunk | while | flops 675742336 | bytes 18889132 | solution.py:191
  82.1 1.2 dynamic_slice.78
  83.9 15.0 %conditional.7 = ((f32[1,8,128,128]{3,2,1,0:T(8,128)}, f32[4096,256]{0,1:T(8,128)})) conditional(s32[]{:T(128)} %convert_element_type.188, (f32[1,8,128,128]{3,2,1,0:T(8,128)}, f32[4096,256]{0,1:T(8,128)}) %tuple.155, (s32[]{:T(128)}, s32[]{:T(128)}, bf16[8,512,256]{2,1,0:T(8,128)(2,1)}, s32[]{:T(128)}, bf16[128,1,8,128]{0,3,2,1:T(8,128)(2,1)}, ...), branch_computations={%region_19.19_spmd, %region_20.20_spmd} | conditional | flops 675742336 | bytes 18888354 | solution.py:182
  85.1 1.6 fusion.33
  86.7 1.4 fusion.34
  88.1 2.1 convolution_bitcast_fusion.2
  90.2 1.5 convolution_bitcast_fusion.1
  91.7 1.3 maximum_add_fusion
  93.1 3.5 dynamic_update_slice.3
  96.6 2.3 fusion.35
  98.9 1.2 dynamic_slice.78
  100.8 1.2 dynamic_slice.78
  102.7 1.2 dynamic_slice.78
  104.5 1.2 dynamic_slice.78
  106.4 1.2 dynamic_slice.78
  108.3 1.2 dynamic_slice.78
  110.2 1.3 dynamic_slice.78
  112.1 4.7 copy.143
  116.8 25.6 %all-gather.10.cloned.1.call-done = f32[256,128,128]{2,1,0:T(8,128)} async-done(((f32[8,128,128]{2,1,0:T(8,128)}), f32[256,128,128]{2,1,0:T(8,128)}) %all-gather.10.cloned.1.call-update) | async-done | bytes 16777232 | tf_op jit(solution)/shard_map/all_gather | solution.py:19
  142.5 58.2 %while.63 = (s32[]{:T(128)}, f32[8,128,128]{2,1,0:T(8,128)S(1)}, s32[]{:T(128)}, f32[32,8]{1,0:T(8,128)}, f32[32,8,128,128]{3,2,1,0:T(8,128)}, /*index=5*/s32[]{:T(128)}, s32[]{:T(128)}) while((s32[]{:T(128)}, f32[8,128,128]{2,1,0:T(8,128)S(1)}, s32[]{:T(128)}, f32[32,8]{1,0:T(8,128)}, f32[32,8,128,128]{3,2,1,0:T(8,128)}, ...), condition=%wide.region_2.3_spmd.clone, body=%wide.region_1.2_spmd.clone.sunk | while | flops 524292 | bytes 1573065 | solution.py:28
  143.2 1.2 fusion.104
  145.1 1.2 fusion.104
  147.0 1.2 fusion.104
  148.8 1.2 fusion.104
  150.7 1.2 fusion.104
  152.6 1.2 fusion.104
  154.5 1.2 fusion.104
  158.2 1.2 fusion.104
  160.1 1.2 fusion.104
  161.9 1.2 fusion.104
  163.8 1.2 fusion.104
  165.7 1.2 fusion.104
  167.6 1.2 fusion.104
  169.4 1.2 fusion.104
  171.3 1.2 fusion.104
  201.6 16.1 %psum.21 = f32[128]{0:T(128)S(1)} all-reduce(f32[128]{0:T(128)S(1)} %get-tuple-element.756), channel_id=1, replica_groups=mesh['ctx'=32,'head'=8] {'head'}, use_global_device_ids=true, to_apply=%region_4.5 | all-reduce | flops 128 | bytes 1024 | tf_op jit(solution)/shard_map/psum | solution.py:97
  217.9 16.0 %psum.22 = f32[128]{0:T(128)S(1)} all-reduce(f32[128]{0:T(128)S(1)} %get-tuple-element.681), channel_id=1, replica_groups=mesh['ctx'=32,'head'=8] {'head'}, use_global_device_ids=true, to_apply=%region_6.7 | all-reduce | flops 128 | bytes 1024 | tf_op jit(solution)/shard_map/psum | solution.py:100
  235.3 124.9 %all-gather.3 = bf16[32,1,8]{2,1,0:T(2,128)(2,1)S(1)} all-gather(bf16[1,1,8]{2,1,0:T(2,128)(2,1)S(1)} %convert_bitcast_fusion), channel_id=1, replica_groups=mesh['ctx'=32,'head'=8] {'ctx'}, dimensions={0}, use_global_device_ids=true | all-gather | bytes 528 | tf_op jit(solution)/shard_map/all_gather | solution.py:36
  360.3 1.4 copy.142
  362.6 1.4 fusion.81
  365.9 66.0 %psum.23 = f32[1024]{0:T(1024)} all-reduce(f32[1024]{0:T(1024)S(1)} %get-tuple-element.680), channel_id=1, replica_groups=mesh['ctx'=32,'head'=8] {'ctx'}, use_global_device_ids=true, to_apply=%region_10.11 | all-reduce | flops 1024 | bytes 8192 | tf_op jit(solution)/shard_map/psum | solution.py:102
  432.2 35.9 %while.60 = (s32[]{:T(128)}, f32[8,128,128]{2,1,0:T(8,128)S(1)}, s32[]{:T(128)}, bf16[32,8,128,128]{3,2,1,0:T(8,128)(2,1)}, bf16[32,8]{1,0:T(8,128)(2,1)S(1)}, /*index=5*/s32[]{:T(128)}, s32[]{:T(128)}, s32[]{:T(128)}, s32[]{:T(128)}) while((s32[]{:T(128)}, f32[8,128,128]{2,1,0:T(8,128)S(1)}, s32[]{:T(128)}, ...), condition=%wide.region_8.9_spmd, body=%wide.region_7.8_spmd.sunk | while | flops 393230 | bytes 1310947 | solution.py:51
  (261 shorter events, 104.0 us)
Async XLA Ops:
  7.2 4.0 copy-start
  7.2 5.2 %copy-start.13 = (bf16[128,1024]{1,0:T(8,128)(2,1)S(1)}, bf16[128,1024]{1,0:T(8,128)(2,1)}, u32[]{:S(2)}) copy-start(bf16[128,1024]{1,0:T(8,128)(2,1)} %param.22) | copy-start | bytes 786436
  7.2 5.5 %copy-start.14 = (bf16[128,1024]{1,0:T(8,128)(2,1)S(1)}, bf16[128,1024]{1,0:T(8,128)(2,1)}, u32[]{:S(2)}) copy-start(bf16[128,1024]{1,0:T(8,128)(2,1)} %param.28) | copy-start | bytes 786436
  7.2 55.2 %all-gather.8.cloned.1.call-start = ((), (), s32[]{:S(2)}) async-start(), calls=%async_computation.1 | async-start | bytes 2162688 | tf_op jit(solution)/shard_map/all_gather | solution.py:255
  8.7 133.7 %all-gather.10.cloned.1.call-start = ((), (), s32[]{:S(2)}) async-start(), calls=%async_computation.3 | async-start | bytes 17301504 | tf_op jit(solution)/shard_map/all_gather | solution.py:19
  9.8 4.8 %copy-start.15 = (bf16[128,1024]{1,0:T(8,128)(2,1)S(1)}, bf16[128,1024]{1,0:T(8,128)(2,1)}, u32[]{:S(2)}) copy-start(bf16[128,1024]{1,0:T(8,128)(2,1)} %param.31) | copy-start | bytes 786436
  11.2 2.4 copy-start.7
  11.2 28.0 %copy-start.10 = (bf16[128,1024]{1,0:T(8,128)(2,1)S(1)}, bf16[128,1024]{1,0:T(8,128)(2,1)}, u32[]{:S(2)}) copy-start(bf16[128,1024]{1,0:T(8,128)(2,1)} %param.23) | copy-start | bytes 786436
  12.2 350.4 %reduce-scatter.2.cloned.1.call-start = ((), (), s32[]{:S(2)}) async-start(), calls=%async_computation.2 | async-start | bytes 2162688 | tf_op jit(solution)/shard_map/reduce_scatter | solution.py:257
  12.5 49.9 %copy-start.5 = (bf16[128,1024]{0,1:T(8,128)(2,1)}, bf16[128,1024]{0,1:T(8,128)(2,1)S(1)}, u32[]{:S(2)}) copy-start(bf16[128,1024]{0,1:T(8,128)(2,1)S(1)} %copy.157) | copy-start | bytes 786436
  39.2 23.2 %copy-start.17 = (pred[128,128]{1,0:T(8,128)(4,1)}, pred[128,128]{1,0:T(8,128)(4,1)S(1)}, u32[]{:S(2)}) copy-start(pred[128,128]{1,0:T(8,128)(4,1)S(1)} %iota_compare_fusion) | copy-start | bytes 49156
  85.1 3.0 copy-start.1
  90.2 1.5 copy-start.3
  91.7 4.9 %copy-start.2 = (bf16[512,256]{1,0:T(8,128)(2,1)S(1)}, bf16[512,256]{1,0:T(8,128)(2,1)}, u32[]{:S(2)}) copy-start(bf16[512,256]{1,0:T(8,128)(2,1)} %copy-done.1) | copy-start | bytes 786436 | tf_op jit(solution)/shard_map/while/body/eval_jaxpr/cond
  116.7 25.7 %copy-start.4 = (f32[8,128,128]{2,1,0:T(8,128)S(1)}, f32[8,128,128]{2,1,0:T(8,128)}, u32[]{:S(2)}) copy-start(f32[8,128,128]{2,1,0:T(8,128)} %custom-call) | copy-start | bytes 1572868
  116.8 315.3 %all-gather.12.cloned.1.call-start = ((), (), s32[]{:S(2)}) async-start(), calls=%async_computation.4 | async-start | bytes 8650752 | tf_op jit(solution)/shard_map/all_gather | solution.py:36
  142.5 58.3 %copy-start.6 = (bf16[128,1024]{0,1:T(8,128)(2,1)S(1)}, bf16[128,1024]{0,1:T(8,128)(2,1)}, u32[]{:S(2)}) copy-start(bf16[128,1024]{0,1:T(8,128)(2,1)} %copy-done.5) | copy-start | bytes 786436
  142.5 58.6 %copy-start.12 = (bf16[8,128,128]{2,1,0:T(8,128)(2,1)S(1)}, bf16[8,128,128]{2,1,0:T(8,128)(2,1)}, u32[]{:S(2)}) copy-start(bf16[8,128,128]{2,1,0:T(8,128)(2,1)} %fusion.53) | copy-start | bytes 786436
  200.7 17.0 %copy-start.9 = (bf16[128,1024]{1,0:T(8,128)(2,1)S(1)}, bf16[128,1024]{1,0:T(8,128)(2,1)}, u32[]{:S(2)}) copy-start(bf16[128,1024]{1,0:T(8,128)(2,1)} %param.27) | copy-start | bytes 786436
  200.7 17.0 %copy-start.16 = (f32[1024]{0:T(1024)S(1)}, f32[1024]{0:T(1024)}, u32[]{:S(2)}) copy-start(f32[1024]{0:T(1024)} %param.26) | copy-start | bytes 12292
  234.1 129.9 %copy-start.18 = (pred[128,128]{1,0:T(8,128)(4,1)S(1)}, pred[128,128]{1,0:T(8,128)(4,1)}, u32[]{:S(2)}) copy-start(pred[128,128]{1,0:T(8,128)(4,1)} %copy-done.17) | copy-start | bytes 49156
  361.7 2.9 copy-start.8
  432.2 35.9 %copy-start.11 = (bf16[128,1024]{1,0:T(8,128)(2,1)S(1)}, bf16[128,1024]{1,0:T(8,128)(2,1)}, u32[]{:S(2)}) copy-start(bf16[128,1024]{1,0:T(8,128)(2,1)} %param.23) | copy-start | bytes 786436
Sparse Core Ops, SparseCore 0:
  11.1 51.1 all-gather.7
  65.5 76.9 all-gather.9
  146.3 186.0 reduce-scatter.1
  335.4 60.6 all-gather.11
where the time goes:
time: 483 us; the launch traced here: 477 us
  blocking collectives  247 us (51%)
  other arithmetic  77 us (16%)
  local copies, waits for them, and re-layouts  62.7 us (13%)
  waiting for transfers between devices  47.9 us (10%)
  matrix products  16.5 us (3%)
  between operations  14.2 us (3%)
  loops' own time  12.4 us (3%)
    all_gather x1, blocking collectives, entering_3(): lax.all_gather(a.astype(kind), axis)  125 us
    psum x1, blocking collectives, lightning_part(): gain_grad = lax.psum(jnp.sum(lin_cot * normed, axis=0), 'ctx')  66 us
    select_n x31, other arithmetic, lap(): jnp.where(position < mine, new, old)  36.4 us
    add x31, other arithmetic, chain_backward(): later[1] + jnp.exp(later[0])[:, None, None] * earlier[1]  34.4 us
    all_gather x1, waiting for transfers between devices, entering_2(): pieces = jax.tree.map(lambda part: lax.all_gather(part, axis), value)  25.6 us
    all_gather x1, blocking collectives, entering_2(): pieces = jax.tree.map(lambda part: lax.all_gather(part, axis), value)  23.6 us
    all_gather x1, waiting for transfers between devices, softmax_part(): lax.all_gather(stacked, 'ctx', axis=0, tiled=True)  22.1 us
    exp x31, local copies, waits for them, and re-layouts, chain_forward(): jnp.exp(later[0])[:, None, None] * earlier[1] + later[1]  21.3 us
  transfers between devices with their start and end apart: 4, of which 2 were waited for; matrix products, arithmetic and copies ran while one was open for 25% of the time, Pallas kernels for 0%

commit v1 on v0

v1 whole, which is shorter than its diff:
```python
import functools
import math

import jax
import jax.numpy as jnp
from jax import lax
from jax.experimental import pallas as pl
from jax.experimental.pallas import tpu as pltpu
from jax.sharding import PartitionSpec as P

D = 128
H = 8
EPS = 1e-06
NEG = -1e30
SCALE = D**-0.5
LOG2E = math.log2(math.e)
F32 = jnp.float32
BF16 = jnp.bfloat16
HIGH = lax.Precision.HIGHEST
MESH = pl.DeviceIdType.MESH


def dot(a, b, ca=1, cb=0, precision=None):
    return lax.dot_general(
        a, b, (((ca,), (cb,)), ((), ())), precision=precision, preferred_element_type=F32
    )


def hs(h):
    return slice(h * D, (h + 1) * D)


def column(row):
    return jnp.broadcast_to(row, (D, D)).T


def kernel(
    n, nh,
    lq, lk, lv, ld, gain, lc, sq, sk, sv, sc,
    o_dq, o_dk, o_dv, o_gg, o_sdq, o_sdk, o_sdv,
    sbuf, dpbuf, kv, pbuf, prec, osend, orec,
    qt, ct, qr, cr, dscb, pb, dqt, m8, l8, d8,
    ms, pw, out, dout, lsend, lrec, esend, erec, wsend, wrec, asend, arec,
    dec, decs, ggs, ggr, pss, psr,
    a2a_s, a2a_r, kv_s, kv_r, pr_s, pr_r, os_s, os_r,
):
    me = lax.axis_index("ctx")
    hd = lax.axis_index("head")
    chip = me // 2
    core = me % 2
    partner = me + 1 - 2 * core
    nc = n // 2
    spn = n // H
    rs = D // spn
    width = H * D

    barrier = pltpu.get_barrier_semaphore()

    @pl.loop(1, n)
    def _(d):
        pl.semaphore_signal(
            barrier, inc=1, device_id={"ctx": lax.rem(me + d, n)}, device_id_type=MESH
        )

    @pl.loop(1, nh)
    def _(d):
        pl.semaphore_signal(
            barrier, inc=1, device_id={"head": lax.rem(hd + d, nh)}, device_id_type=MESH
        )

    kv[chip, core, 0] = sk[...]
    kv[chip, core, 1] = sv[...]

    row_i = lax.broadcasted_iota(jnp.int32, (D, D), 0)
    col_i = lax.broadcasted_iota(jnp.int32, (D, D), 1)
    causal = col_i <= row_i
    tri = jnp.where(causal, 1.0, 0.0).astype(F32)
    ldv = ld[...]
    cum = dot(tri, ldv, 1, 0, HIGH)
    cum_t = dot(ldv, tri, 0, 1, HIGH)
    kdec = jnp.exp(cum[D - 1 : D, :] - cum)
    qdec = jnp.exp(cum)
    tot_t = jnp.exp(cum_t[:, D - 1 : D])

    def col(a, h):
        return jnp.broadcast_to(a[:, h : h + 1], (D, D))

    for h in range(H):
        kd = (lk[:, hs(h)].astype(F32) * col(kdec, h)).astype(BF16)
        local = dot(kd, lv[:, hs(h)], 0, 0)
        lsend[h * spn : (h + 1) * spn] = local.astype(BF16).reshape(spn, rs, D)
        dec[h] = jnp.broadcast_to(tot_t[h : h + 1, :], (1, D))
    lrec[me] = lsend[me]
    decs[me] = dec[me // spn]

    pl.semaphore_wait(barrier, n - 1 + nh - 1)

    def exchange(src, dst, k, by_target=True, pick=None):
        @pl.loop(1, n)
        def _(d):
            to = lax.rem(me + d, n)
            if pick is not None:
                s = src.at[pick(to)]
            else:
                s = src.at[to] if by_target else src
            pltpu.make_async_remote_copy(
                src_ref=s,
                dst_ref=dst.at[me],
                send_sem=a2a_s.at[k],
                recv_sem=a2a_r.at[k],
                device_id={"ctx": to},
                device_id_type=MESH,
            ).start()

    def arrived(dst, k, count):
        part = dst.at[pl.ds(0, count)]
        pltpu.make_async_copy(part, part, a2a_r.at[k]).wait()

    def left(dst, k, count):
        part = dst.at[pl.ds(0, count)]
        pltpu.make_async_copy(part, part, a2a_s.at[k]).wait()

    exchange(lsend, lrec, 0)
    exchange(dec, decs, 1, pick=lambda to: to // spn)

    def kv_copy(k, par, sem, to):
        return pltpu.make_async_remote_copy(
            src_ref=kv.at[k, par],
            dst_ref=kv.at[k, par],
            send_sem=kv_s.at[sem],
            recv_sem=kv_r.at[k, par],
            device_id={"ctx": to},
            device_id_type=MESH,
        )

    def kv_send():
        kv_copy(chip, core, chip, partner).start()

        @pl.loop(chip + 1, nc)
        def _(k):
            kv_copy(chip, core, k, 2 * k + core).start()

    def kv_wait(k, par):
        part = kv.at[k, par]
        pltpu.make_async_copy(part, part, kv_r.at[k, par]).wait()

    def kv_relay():
        @pl.loop(0, chip)
        def _(i):
            k = chip - 1 - i
            kv_wait(k, core)
            kv_copy(k, core, k, partner).start()

    kv_send()

    for h in range(H):
        gap = col(cum, h) - jnp.broadcast_to(cum_t[h : h + 1, :], (D, D))
        m = jnp.where(causal, jnp.exp(jnp.minimum(gap, 0.0)), 0.0) * SCALE
        ms[h] = m
        p = (dot(lq[:, hs(h)], lk[:, hs(h)], 1, 1) * m).astype(BF16)
        pw[h] = p
        out[:, hs(h)] = dot(p, lv[:, hs(h)])

    m8[...] = jnp.full((8, width), NEG, F32)
    for h in range(H):
        qh = sq[:, hs(h)]
        chh = sc[:, hs(h)]
        qt[:, hs(h)] = qh.T
        ct[:, hs(h)] = chh.T

    arrived(lrec, 0, n - 1)
    arrived(decs, 1, n - 1)
    run = jnp.zeros((rs, D), F32)
    for c in range(n):
        esend[c] = run.astype(BF16)
        run = jnp.broadcast_to(decs[c], (rs, D)) * run + lrec[c].astype(F32)
    erec[me] = esend[me]
    exchange(esend, erec, 2)

    kv_relay()

    def scores(k, masked):
        keys = kv[k, :, 0].reshape(2 * D, D)
        vals = kv[k, :, 1].reshape(2 * D, D)
        for j in range(width // 256):
            lanes = slice(j * 256, (j + 1) * 256)
            s = dot(keys, qt[:, lanes])
            if masked:
                kpos = lax.broadcasted_iota(jnp.int32, (2 * D, 256), 0)
                qpos = core * D + lax.broadcasted_iota(jnp.int32, (2 * D, 256), 1) % D
                s = jnp.where(kpos <= qpos, s, NEG)
            sbuf[k, :, lanes] = s
            m8[:, lanes] = jnp.maximum(m8[:, lanes], jnp.max(s.reshape(2 * D // 8, 8, 256), axis=0))
            dpbuf[k, :, lanes] = dot(vals, ct[:, lanes])

    kv_wait(chip, 1 - core)
    scores(chip, True)

    arrived(erec, 2, n - 1)

    def state(ref, h):
        return ref[h * spn : (h + 1) * spn].reshape(D, D)

    sum_sq = jnp.zeros((D, D), F32)
    sum_x = jnp.zeros((D, D), F32)
    for h in range(H):
        o = out[:, hs(h)] + (SCALE * col(qdec, h)) * dot(lq[:, hs(h)], state(erec, h))
        out[:, hs(h)] = o
        sum_sq += o * o
        sum_x += lc[:, hs(h)].astype(F32) * gain[:, hs(h)] * o
    ones = jnp.ones((8, D), F32)
    pss[0] = dot(ones, sum_sq, 1, 1, HIGH)
    pss[1] = dot(ones, sum_x, 1, 1, HIGH)
    psr[hd] = pss[...]

    @pl.loop(1, nh)
    def _(d):
        to = lax.rem(hd + d, nh)
        pltpu.make_async_remote_copy(
            src_ref=pss,
            dst_ref=psr.at[hd],
            send_sem=a2a_s.at[3],
            recv_sem=a2a_r.at[3],
            device_id={"head": to},
            device_id_type=MESH,
        ).start()

    @pl.loop(0, chip // 2)
    def _(i):
        k = chip - 1 - i
        kv_wait(k, 1 - core)
        scores(k, False)

    arrived(psr, 3, nh - 1)
    sums = jnp.sum(psr[...], axis=0)
    inv = lax.rsqrt(sums[0, 0:1] / (nh * width) + EPS)
    cross = sums[1, 0:1] * inv / (nh * width)
    inv_c = column(inv)
    cross_c = column(cross)
    for h in range(H):
        normed = out[:, hs(h)] * inv_c
        cot = lc[:, hs(h)].astype(F32)
        do = ((cot * gain[:, hs(h)] - normed * cross_c) * inv_c).astype(BF16)
        dout[:, hs(h)] = do
        ggs[h : h + 1, :] = jnp.sum(cot * normed, axis=0, keepdims=True)
        qd = (lq[:, hs(h)].astype(F32) * col(qdec, h)).astype(BF16)
        wsend[h * spn : (h + 1) * spn] = dot(qd, do, 0, 0).astype(BF16).reshape(spn, rs, D)
    wrec[me] = wsend[me]
    ggr[me] = ggs[...]
    exchange(wsend, wrec, 4)
    exchange(ggs, ggr, 5, by_target=False)

    for h in range(H):
        do = dout[:, hs(h)]
        dp = (dot(do, lv[:, hs(h)], 1, 1) * ms[h]).astype(BF16)
        o_dq[:, hs(h)] = dot(dp, lk[:, hs(h)]) + (SCALE * col(qdec, h)) * dot(do, state(erec, h), 1, 1)
        o_dk[:, hs(h)] = dot(dp, lq[:, hs(h)], 0, 0)
        o_dv[:, hs(h)] = dot(pw[h], do, 0, 0)

    arrived(wrec, 4, n - 1)
    run = jnp.zeros((rs, D), F32)
    for c in range(n - 1, -1, -1):
        asend[c] = run.astype(BF16)
        run = jnp.broadcast_to(decs[c], (rs, D)) * run + wrec[c].astype(F32)
    arec[me] = asend[me]
    exchange(asend, arec, 6)

    @pl.loop(chip // 2, chip)
    def _(i):
        k = chip - 1 - i
        kv_wait(k, 1 - core)
        scores(k, False)

    factor = SCALE * LOG2E
    top = jnp.max(m8[...], axis=0, keepdims=True) * factor
    l8[...] = jnp.zeros((8, width), F32)
    d8[...] = jnp.zeros((8, width), F32)

    @pl.loop(0, chip + 1)
    def _(k):
        for j in range(width // 256):
            lanes = slice(j * 256, (j + 1) * 256)
            p = jnp.exp2(sbuf[k, :, lanes] * factor - top[:, lanes])
            sbuf[k, :, lanes] = p
            l8[:, lanes] += jnp.sum(p.reshape(2 * D // 8, 8, 256), axis=0)
            d8[:, lanes] += jnp.sum((p * dpbuf[k, :, lanes]).reshape(2 * D // 8, 8, 256), axis=0)

    rinv = 1.0 / jnp.sum(l8[...], axis=0, keepdims=True)
    delta = jnp.sum(d8[...], axis=0, keepdims=True) * rinv
    for h in range(H):
        rc = column(rinv[:, hs(h)])
        qr[h * D : (h + 1) * D, :] = (sq[:, hs(h)].astype(F32) * (rc * SCALE)).astype(BF16)
        cr[h * D : (h + 1) * D, :] = (sc[:, hs(h)].astype(F32) * rc).astype(BF16)

    arrived(arec, 6, n - 1)
    for h in range(H):
        a = state(arec, h)
        kd = SCALE * col(kdec, h)
        o_dk[:, hs(h)] += kd * dot(lv[:, hs(h)], a, 1, 1)
        o_dv[:, hs(h)] += kd * dot(lk[:, hs(h)], a)

    dqt[...] = jnp.zeros((D, width), F32)

    def pair_copy(k):
        return pltpu.make_async_remote_copy(
            src_ref=pbuf.at[k, 1 - core],
            dst_ref=prec.at[k],
            send_sem=pr_s.at[k],
            recv_sem=pr_r.at[k],
            device_id={"ctx": partner},
            device_id_type=MESH,
        )

    def own_copy(k):
        return pltpu.make_async_remote_copy(
            src_ref=osend.at[k],
            dst_ref=orec.at[chip],
            send_sem=os_s.at[k],
            recv_sem=os_r.at[chip],
            device_id={"ctx": 2 * k + core},
            device_id_type=MESH,
        )

    def own_send(k):
        pltpu.make_async_copy(prec.at[k], prec.at[k], pr_r.at[k]).wait()
        osend[k] = (pbuf[k, core].astype(F32) + prec[k].astype(F32)).astype(BF16)
        own_copy(k).start()

    @pl.loop(0, chip + 1)
    def _(k):
        keys = kv[k, :, 0].reshape(2 * D, D)
        for j in range(width // 256):
            lanes = slice(j * 256, (j + 1) * 256)
            p = sbuf[k, :, lanes]
            pb[:, lanes] = p.astype(BF16)
            ds = (p * (dpbuf[k, :, lanes] - delta[:, lanes])).astype(BF16)
            dscb[:, lanes] = ds
            dqt[:, lanes] += dot(keys, ds, 0, 0)
        dk = dot(dscb[...], qr[...])
        dv = dot(pb[...], cr[...])
        pbuf[k, :, 0] = dk.astype(BF16).reshape(2, D, D)
        pbuf[k, :, 1] = dv.astype(BF16).reshape(2, D, D)
        pair_copy(k).start()

        @pl.when(k > 0)
        def _():
            own_send(k - 1)

    for h in range(H):
        o_sdq[:, hs(h)] = (dqt[:, hs(h)] * (rinv[:, hs(h)] * SCALE)).T

    arrived(ggr, 5, n - 1)
    o_gg[...] = jnp.sum(ggr[...], axis=0)

    pltpu.make_async_copy(prec.at[chip], prec.at[chip], pr_r.at[chip]).wait()
    o_sdk[...] = pbuf[chip, core, 0].astype(F32) + prec[chip, 0].astype(F32)
    o_sdv[...] = pbuf[chip, core, 1].astype(F32) + prec[chip, 1].astype(F32)

    @pl.loop(chip + 1, nc)
    def _(k):
        pltpu.make_async_copy(orec.at[k], orec.at[k], os_r.at[k]).wait()
        o_sdk[...] += orec[k, 0].astype(F32)
        o_sdv[...] += orec[k, 1].astype(F32)

    left(lsend, 0, n - 1)
    left(decs, 1, n - 1)
    left(esend, 2, n - 1)
    left(psr, 3, nh - 1)
    left(wsend, 4, n - 1)
    left(ggr, 5, n - 1)
    left(asend, 6, n - 1)

    @pl.loop(0, nc)
    def _(k):
        pltpu.make_async_copy(kv.at[0, 0], kv.at[0, 0], kv_s.at[k]).wait()

    @pl.loop(0, chip + 1)
    def _(k):
        pltpu.make_async_copy(prec.at[k], prec.at[k], pr_s.at[k]).wait()

    @pl.loop(0, chip)
    def _(k):
        pltpu.make_async_copy(osend.at[k], osend.at[k], os_s.at[k]).wait()


def on_device(n, nh, lq, lk, lv, ld, gain, lc, sq, sk, sv, sc):
    nc = n // 2
    spn = n // H
    rs = D // spn
    width = H * D
    state = pltpu.VMEM((n, rs, D), BF16)
    scratch = [
        pltpu.VMEM((nc, 2 * D, width), F32),
        pltpu.VMEM((nc, 2 * D, width), F32),
        pltpu.VMEM((nc, 2, 2, D, D), BF16),
        pltpu.VMEM((nc, 2, 2, D, D), BF16),
        pltpu.VMEM((nc, 2, D, D), BF16),
        pltpu.VMEM((nc, 2, D, D), BF16),
        pltpu.VMEM((nc, 2, D, D), BF16),
        pltpu.VMEM((D, width), BF16),
        pltpu.VMEM((D, width), BF16),
        pltpu.VMEM((width, D), BF16),
        pltpu.VMEM((width, D), BF16),
        pltpu.VMEM((2 * D, width), BF16),
        pltpu.VMEM((2 * D, width), BF16),
        pltpu.VMEM((D, width), F32),
        pltpu.VMEM((8, width), F32),
        pltpu.VMEM((8, width), F32),
        pltpu.VMEM((8, width), F32),
        pltpu.VMEM((H, D, D), F32),
        pltpu.VMEM((H, D, D), BF16),
        pltpu.VMEM((D, width), F32),
        pltpu.VMEM((D, width), BF16),
        *([state] * 8),
        pltpu.VMEM((H, 1, D), F32),
        pltpu.VMEM((n, 1, D), F32),
        pltpu.VMEM((H, D), F32),
        pltpu.VMEM((n, H, D), F32),
        pltpu.VMEM((2, 8, D), F32),
        pltpu.VMEM((nh, 2, 8, D), F32),
        pltpu.SemaphoreType.DMA((7,)),
        pltpu.SemaphoreType.DMA((7,)),
        pltpu.SemaphoreType.DMA((nc,)),
        pltpu.SemaphoreType.DMA((nc, 2)),
        pltpu.SemaphoreType.DMA((nc,)),
        pltpu.SemaphoreType.DMA((nc,)),
        pltpu.SemaphoreType.DMA((nc,)),
        pltpu.SemaphoreType.DMA((nc,)),
    ]
    big = jax.ShapeDtypeStruct((D, width), F32)
    small = jax.ShapeDtypeStruct((D, D), F32)
    vmem = pl.BlockSpec(memory_space=pltpu.VMEM)
    res = pl.pallas_call(
        functools.partial(kernel, n, nh),
        out_shape=(big, big, big, jax.ShapeDtypeStruct((H, D), F32), big, small, small),
        in_specs=[vmem] * 10,
        out_specs=(vmem,) * 7,
        scratch_shapes=scratch,
        compiler_params=pltpu.CompilerParams(
            collective_id=0, has_side_effects=True, vmem_limit_bytes=62 * 1024 * 1024
        ),
        name="grads",
    )(lq, lk, lv, ld, gain.reshape(1, width), lc, sq, sk, sv, sc)
    dq, dk, dv, gg, sdq, sdk, sdv = res
    return dq, dk, dv, gg.reshape(width), sdq, sdk, sdv


def solution(mesh):
    n, nh = mesh.shape["ctx"], mesh.shape["head"]
    both = P("ctx", "head")
    return jax.shard_map(
        functools.partial(on_device, n, nh),
        mesh=mesh,
        in_specs=(both, both, both, both, P("head"), both, both, both, both, both),
        out_specs=(both, both, both, P("head"), both, both, both),
        check_vma=False,
    )
```

time: 483 us -> 82.5 us (0.17)
  the two profiles are of different devices: /device:TPU:32 before, /device:TPU:26 now
where the time goes in v1:
time: 82.5 us; the launch traced here: 82.2 us
  Pallas kernels  73.2 us (89%)
  local copies, waits for them, and re-layouts  8.34 us (10%)
    pallas_call x1, Pallas kernels, on_device(): pl.pallas_call(functools.partial(kernel, n, nh), out_shape=(big, big, big...  73.2 us
    unnamed x20, local copies, waits for them, and re-layouts  8.34 us

profile of v1, /device:TPU:26, one launch (start us, length us, event | category | flops | bytes accessed | tf_op | source)
XLA Modules:
  0.0 82.2 jit_solution(14044844651242345191)
XLA Ops:
  0.6 1.4 %copy.17.ld = f32[128,8]{1,0:T(8,128)} copy(f32[128,8]{0,1:T(8,128)} %param.13) | data formatting | bytes 8192 | tf_op args[3]
  2.0 73.2 %grads.1 = (f32[128,1024]{1,0:T(8,128)}, f32[128,1024]{1,0:T(8,128)}, f32[128,1024]{1,0:T(8,128)}, f32[8,128]{1,0:T(8,128)}, f32[128,1024]{1,0:T(8,128)}, /*index=5*/f32[128,128]{1,0:T(8,128)}, f32[128,128]{1,0:T(8,128)}) custom-call(bf16[128,1024]{1,0:T(8,128)(2,1)} %lq.1, bf16[128,1024]{1,0:T(8,128)(2,1)} %lk.1, bf16[128,1024]{1,0:T(8,128)(2,1)} %lv.1, ...), custom_call_target="tpu_custom_call" | custom-call | tf_op jit(solution)/shard_map/grads/pallas_call | solution.py:433
  75.2 0.0 copy-start.2
  75.2 1.9 %copy.25 = f32[128,1024]{1,0:T(8,128)} copy(f32[128,1024]{1,0:T(8,128)} %get-tuple-element.28) | data formatting | bytes 1048576
  77.2 0.0 copy-done.2
  77.2 0.0 copy-start.1
  77.2 0.8 copy.26
  78.0 0.4 copy-done.1
  78.4 0.0 copy-start.5
  78.4 0.0 copy-start
  78.4 0.8 copy.27
  79.2 0.0 copy-done.5
  79.2 0.6 copy.28
  79.8 0.0 copy-done
  79.8 0.0 copy-start.4
  79.8 0.8 copy.29
  80.6 0.1 copy-done.4
  80.7 0.0 copy-start.3
  80.7 0.6 copy.30
  81.3 0.2 copy-done.3
  81.6 0.6 copy.31
Async XLA Ops:
  75.2 2.0 %copy-start.2 = (f32[128,1024]{1,0:T(8,128)S(1)}, f32[128,1024]{1,0:T(8,128)}, u32[]{:S(2)}) copy-start(f32[128,1024]{1,0:T(8,128)} %get-tuple-element.29) | copy-start | bytes 1572868
  77.2 1.2 %copy-start.1 = (f32[128,1024]{1,0:T(8,128)S(1)}, f32[128,1024]{1,0:T(8,128)}, u32[]{:S(2)}) copy-start(f32[128,1024]{1,0:T(8,128)} %get-tuple-element.30) | copy-start | bytes 1572868
  78.4 0.8 copy-start.5
  78.4 1.4 %copy-start = (f32[128,1024]{1,0:T(8,128)S(1)}, f32[128,1024]{1,0:T(8,128)}, u32[]{:S(2)}) copy-start(f32[128,1024]{1,0:T(8,128)} %get-tuple-element.32) | copy-start | bytes 1572868
  79.8 0.9 %copy-start.4 = (f32[128,128]{1,0:T(8,128)S(1)}, f32[128,128]{1,0:T(8,128)}, u32[]{:S(2)}) copy-start(f32[128,128]{1,0:T(8,128)} %get-tuple-element.33) | copy-start | bytes 196612
  80.7 0.9 %copy-start.3 = (f32[128,128]{1,0:T(8,128)S(1)}, f32[128,128]{1,0:T(8,128)}, u32[]{:S(2)}) copy-start(f32[128,128]{1,0:T(8,128)} %get-tuple-element.34) | copy-start | bytes 196612

commit v2 on v1

--- a/solution.py
+++ b/solution.py
@@ -35,14 +35,14 @@
 
 
 def kernel(
-    n, nh,
+    n, nh, gy,
     lq, lk, lv, ld, gain, lc, sq, sk, sv, sc,
     o_dq, o_dk, o_dv, o_gg, o_sdq, o_sdk, o_sdv,
-    sbuf, dpbuf, kv, pbuf, prec, osend, orec,
+    sbuf, dpbuf, kv, pbuf, prec, osend, orec, xsend, xrec, acc,
     qt, ct, qr, cr, dscb, pb, dqt, m8, l8, d8,
     ms, pw, out, dout, lsend, lrec, esend, erec, wsend, wrec, asend, arec,
     dec, decs, ggs, ggr, pss, psr,
-    a2a_s, a2a_r, kv_s, kv_r, pr_s, pr_r, os_s, os_r,
+    a2a_s, a2a_r, kv_s, kv_f, kv_r, pr_s, pr_r, os_s, os_r, xs_s, xs_r,
 ):
     me = lax.axis_index("ctx")
     hd = lax.axis_index("head")
@@ -50,6 +50,8 @@
     core = me % 2
     partner = me + 1 - 2 * core
     nc = n // 2
+    gx = nc // gy
+    cx, cy = chip // gy, chip % gy
     spn = n // H
     rs = D // spn
     width = H * D
@@ -76,8 +78,8 @@
     causal = col_i <= row_i
     tri = jnp.where(causal, 1.0, 0.0).astype(F32)
     ldv = ld[...]
-    cum = dot(tri, ldv, 1, 0, HIGH)
-    cum_t = dot(ldv, tri, 0, 1, HIGH)
+    cum = dot(tri, ldv, 1, 1, HIGH)
+    cum_t = dot(ldv, tri, 1, 1, HIGH)
     kdec = jnp.exp(cum[D - 1 : D, :] - cum)
     qdec = jnp.exp(cum)
     tot_t = jnp.exp(cum_t[:, D - 1 : D])
@@ -123,22 +125,42 @@
     exchange(lsend, lrec, 0)
     exchange(dec, decs, 1, pick=lambda to: to // spn)
 
-    def kv_copy(k, par, sem, to):
+    def kv_copy(k, sem, to):
         return pltpu.make_async_remote_copy(
-            src_ref=kv.at[k, par],
-            dst_ref=kv.at[k, par],
-            send_sem=kv_s.at[sem],
-            recv_sem=kv_r.at[k, par],
+            src_ref=kv.at[k, core],
+            dst_ref=kv.at[k, core],
+            send_sem=sem,
+            recv_sem=kv_r.at[k, core],
             device_id={"ctx": to},
             device_id_type=MESH,
         )
 
     def kv_send():
-        kv_copy(chip, core, chip, partner).start()
-
-        @pl.loop(chip + 1, nc)
-        def _(k):
-            kv_copy(chip, core, k, 2 * k + core).start()
+        kv_copy(chip, kv_s.at[chip], partner).start()
+
+        @pl.loop(cx + 1, gx)
+        def _(x):
+            k = x * gy + cy
+            kv_copy(chip, kv_f.at[k], 2 * k + core).start()
+
+        @pl.loop(cy + 1, gy)
+        def _(y):
+            k = cx * gy + y
+            kv_copy(chip, kv_f.at[k], 2 * k + core).start()
+
+    def kv_spread():
+        @pl.loop(0, cx)
+        def _(i):
+            x = cx - 1 - i
+            k = x * gy + cy
+            kv_wait(k, core)
+
+            @pl.loop(1, gy)
+            def _(d):
+                y = lax.rem(cy + d, gy)
+                kv_copy(k, kv_f.at[x * gy + y], 2 * (cx * gy + y) + core).start()
+
+            kv_copy(k, kv_s.at[k], partner).start()
 
     def kv_wait(k, par):
         part = kv.at[k, par]
@@ -148,8 +170,11 @@
         @pl.loop(0, chip)
         def _(i):
             k = chip - 1 - i
-            kv_wait(k, core)
-            kv_copy(k, core, k, partner).start()
+
+            @pl.when(k % gy != cy)
+            def _():
+                kv_wait(k, core)
+                kv_copy(k, kv_s.at[k], partner).start()
 
     kv_send()
 
@@ -176,8 +201,7 @@
         run = jnp.broadcast_to(decs[c], (rs, D)) * run + lrec[c].astype(F32)
     erec[me] = esend[me]
     exchange(esend, erec, 2)
-
-    kv_relay()
+    kv_spread()
 
     def scores(k, masked):
         keys = kv[k, :, 0].reshape(2 * D, D)
@@ -225,6 +249,8 @@
             device_id_type=MESH,
         ).start()
 
+    kv_relay()
+
     @pl.loop(0, chip // 2)
     def _(i):
         k = chip - 1 - i
@@ -311,20 +337,34 @@
             device_id_type=MESH,
         )
 
-    def own_copy(k):
+    def y_copy(k):
+        x, y = k // gy, k % gy
         return pltpu.make_async_remote_copy(
             src_ref=osend.at[k],
-            dst_ref=orec.at[chip],
+            dst_ref=orec.at[x, cy],
             send_sem=os_s.at[k],
-            recv_sem=os_r.at[chip],
-            device_id={"ctx": 2 * k + core},
+            recv_sem=os_r.at[x, cy],
+            device_id={"ctx": 2 * (cx * gy + y) + core},
+            device_id_type=MESH,
+        )
+
+    def x_copy(x):
+        return pltpu.make_async_remote_copy(
+            src_ref=xsend.at[x],
+            dst_ref=xrec.at[cx],
+            send_sem=xs_s.at[x],
+            recv_sem=xs_r.at[cx],
+            device_id={"ctx": 2 * (x * gy + cy) + core},
             device_id_type=MESH,
         )
 
     def own_send(k):
         pltpu.make_async_copy(prec.at[k], prec.at[k], pr_r.at[k]).wait()
         osend[k] = (pbuf[k, core].astype(F32) + prec[k].astype(F32)).astype(BF16)
-        own_copy(k).start()
+
+        @pl.when(k % gy != cy)
+        def _():
+            y_copy(k).start()
 
     @pl.loop(0, chip + 1)
     def _(k):
@@ -352,15 +392,35 @@
     arrived(ggr, 5, n - 1)
     o_gg[...] = jnp.sum(ggr[...], axis=0)
 
+    def y_add(x, y):
+        pltpu.make_async_copy(orec.at[x, y], orec.at[x, y], os_r.at[x, y]).wait()
+        acc[...] += orec[x, y].astype(F32)
+
+    @pl.loop(0, cx)
+    def _(x):
+        acc[...] = osend[x * gy + cy].astype(F32)
+
+        @pl.loop(1, gy)
+        def _(d):
+            y_add(x, lax.rem(cy + d, gy))
+
+        xsend[x] = acc[...].astype(BF16)
+        x_copy(x).start()
+
     pltpu.make_async_copy(prec.at[chip], prec.at[chip], pr_r.at[chip]).wait()
-    o_sdk[...] = pbuf[chip, core, 0].astype(F32) + prec[chip, 0].astype(F32)
-    o_sdv[...] = pbuf[chip, core, 1].astype(F32) + prec[chip, 1].astype(F32)
-
-    @pl.loop(chip + 1, nc)
-    def _(k):
-        pltpu.make_async_copy(orec.at[k], orec.at[k], os_r.at[k]).wait()
-        o_sdk[...] += orec[k, 0].astype(F32)
-        o_sdv[...] += orec[k, 1].astype(F32)
+    acc[...] = pbuf[chip, core].astype(F32) + prec[chip].astype(F32)
+
+    @pl.loop(cy + 1, gy)
+    def _(y):
+        y_add(cx, y)
+
+    @pl.loop(cx + 1, gx)
+    def _(x):
+        pltpu.make_async_copy(xrec.at[x], xrec.at[x], xs_r.at[x]).wait()
+        acc[...] += xrec[x].astype(F32)
+
+    o_sdk[...] = acc[0]
+    o_sdv[...] = acc[1]
 
     left(lsend, 0, n - 1)
     left(decs, 1, n - 1)
@@ -372,7 +432,16 @@
 
     @pl.loop(0, nc)
     def _(k):
-        pltpu.make_async_copy(kv.at[0, 0], kv.at[0, 0], kv_s.at[k]).wait()
+        @pl.when(k <= chip)
+        def _():
+            pltpu.make_async_copy(kv.at[0, 0], kv.at[0, 0], kv_s.at[k]).wait()
+
+        x, y = k // gy, k % gy
+        sent = ((x < cx) & (y != cy)) | ((x == cx) & (y > cy)) | ((x > cx) & (y == cy))
+
+        @pl.when(sent)
+        def _():
+            pltpu.make_async_copy(kv.at[0, 0], kv.at[0, 0], kv_f.at[k]).wait()
 
     @pl.loop(0, chip + 1)
     def _(k):
@@ -380,11 +449,27 @@
 
     @pl.loop(0, chip)
     def _(k):
-        pltpu.make_async_copy(osend.at[k], osend.at[k], os_s.at[k]).wait()
+        @pl.when(k % gy != cy)
+        def _():
+            pltpu.make_async_copy(osend.at[k], osend.at[k], os_s.at[k]).wait()
+
+    @pl.loop(0, cx)
+    def _(x):
+        pltpu.make_async_copy(xsend.at[x], xsend.at[x], xs_s.at[x]).wait()
+
+
+def finish(*refs):
+    copies = [pltpu.make_async_copy(refs[i], refs[7 + i], refs[14].at[i]) for i in range(7)]
+    for copy in copies:
+        copy.start()
+    for copy in copies:
+        copy.wait()
 
 
 def on_device(n, nh, lq, lk, lv, ld, gain, lc, sq, sk, sv, sc):
     nc = n // 2
+    gy = math.isqrt(nc)
+    gx = nc // gy
     spn = n // H
     rs = D // spn
     width = H * D
@@ -396,7 +481,10 @@
         pltpu.VMEM((nc, 2, 2, D, D), BF16),
         pltpu.VMEM((nc, 2, D, D), BF16),
         pltpu.VMEM((nc, 2, D, D), BF16),
-        pltpu.VMEM((nc, 2, D, D), BF16),
+        pltpu.VMEM((gx, gy, 2, D, D), BF16),
+        pltpu.VMEM((gx, 2, D, D), BF16),
+        pltpu.VMEM((gx, 2, D, D), BF16),
+        pltpu.VMEM((2, D, D), F32),
         pltpu.VMEM((D, width), BF16),
         pltpu.VMEM((D, width), BF16),
         pltpu.VMEM((width, D), BF16),
@@ -421,27 +509,38 @@
         pltpu.SemaphoreType.DMA((7,)),
         pltpu.SemaphoreType.DMA((7,)),
         pltpu.SemaphoreType.DMA((nc,)),
+        pltpu.SemaphoreType.DMA((nc,)),
         pltpu.SemaphoreType.DMA((nc, 2)),
         pltpu.SemaphoreType.DMA((nc,)),
         pltpu.SemaphoreType.DMA((nc,)),
         pltpu.SemaphoreType.DMA((nc,)),
-        pltpu.SemaphoreType.DMA((nc,)),
+        pltpu.SemaphoreType.DMA((gx, gy)),
+        pltpu.SemaphoreType.DMA((gx,)),
+        pltpu.SemaphoreType.DMA((gx,)),
     ]
     big = jax.ShapeDtypeStruct((D, width), F32)
     small = jax.ShapeDtypeStruct((D, D), F32)
     vmem = pl.BlockSpec(memory_space=pltpu.VMEM)
     res = pl.pallas_call(
-        functools.partial(kernel, n, nh),
+        functools.partial(kernel, n, nh, gy),
         out_shape=(big, big, big, jax.ShapeDtypeStruct((H, D), F32), big, small, small),
         in_specs=[vmem] * 10,
         out_specs=(vmem,) * 7,
         scratch_shapes=scratch,
         compiler_params=pltpu.CompilerParams(
-            collective_id=0, has_side_effects=True, vmem_limit_bytes=62 * 1024 * 1024
+            collective_id=0, has_side_effects=True, vmem_limit_bytes=48 * 1024 * 1024
         ),
         name="grads",
-    )(lq, lk, lv, ld, gain.reshape(1, width), lc, sq, sk, sv, sc)
-    dq, dk, dv, gg, sdq, sdk, sdv = res
+    )(lq, lk, lv, ld.T, gain.reshape(1, width), lc, sq, sk, sv, sc)
+    dq, dk, dv, gg, sdq, sdk, sdv = pl.pallas_call(
+        finish,
+        out_shape=tuple(jax.ShapeDtypeStruct(r.shape, r.dtype) for r in res),
+        in_specs=[vmem] * 7,
+        out_specs=(pl.BlockSpec(memory_space=pl.ANY),) * 7,
+        scratch_shapes=[pltpu.SemaphoreType.DMA((7,))],
+        compiler_params=pltpu.CompilerParams(vmem_limit_bytes=8 * 1024 * 1024),
+        name="finish",
+    )(*res)
     return dq, dk, dv, gg.reshape(width), sdq, sdk, sdv
 
 

time: 82.5 us -> 74.7 us (0.905)
  Pallas kernels: 73.2 us -> 64.7 us
    pallas_call x1 -> x2, Pallas kernels: 73.2 us -> 64.7 us  [the longest x1 63.3 us: on_device(): pl.pallas_call(functools.partial(kernel, n, nh, gy), out_shape=(big, big,...]
where the time goes in v2:
time: 74.7 us; the launch traced here: 74 us
  Pallas kernels  64.7 us (87%)
  local copies, waits for them, and re-layouts  8.58 us (11%)
    pallas_call x1, Pallas kernels, on_device(): pl.pallas_call(functools.partial(kernel, n, nh, gy), out_shape=(big, big,...  63.3 us
    unnamed x20, local copies, waits for them, and re-layouts  8.58 us

profile of v2, /device:TPU:26, one launch (start us, length us, event | category | flops | bytes accessed | tf_op | source)
XLA Modules:
  0.0 74.0 jit_solution(3824873008268177841)
XLA Ops:
  0.6 0.0 copy-start
  0.6 0.9 %copy-done = bf16[128,1024]{1,0:T(8,128)(2,1)S(1)} copy-done((bf16[128,1024]{1,0:T(8,128)(2,1)S(1)}, bf16[128,1024]{1,0:T(8,128)(2,1)}, u32[]{:S(2)}) %copy-start) | copy-done | bytes 262168
  1.6 0.0 copy-start.1
  1.6 0.9 %copy-done.1 = bf16[128,1024]{1,0:T(8,128)(2,1)S(1)} copy-done((bf16[128,1024]{1,0:T(8,128)(2,1)S(1)}, bf16[128,1024]{1,0:T(8,128)(2,1)}, u32[]{:S(2)}) %copy-start.1) | copy-done | bytes 262168
  2.5 0.0 copy-start.2
  2.5 0.9 %copy-done.2 = bf16[128,1024]{1,0:T(8,128)(2,1)S(1)} copy-done((bf16[128,1024]{1,0:T(8,128)(2,1)S(1)}, bf16[128,1024]{1,0:T(8,128)(2,1)}, u32[]{:S(2)}) %copy-start.2) | copy-done | bytes 262168
  3.5 0.0 copy-start.3
  3.5 0.9 %copy-done.3 = bf16[128,1024]{1,0:T(8,128)(2,1)S(1)} copy-done((bf16[128,1024]{1,0:T(8,128)(2,1)S(1)}, bf16[128,1024]{1,0:T(8,128)(2,1)}, u32[]{:S(2)}) %copy-start.3) | copy-done | bytes 262168
  4.4 0.0 copy-start.4
  4.4 0.9 %copy-done.4 = bf16[128,1024]{1,0:T(8,128)(2,1)S(1)} copy-done((bf16[128,1024]{1,0:T(8,128)(2,1)S(1)}, bf16[128,1024]{1,0:T(8,128)(2,1)}, u32[]{:S(2)}) %copy-start.4) | copy-done | bytes 262168
  5.4 0.0 copy-start.5
  5.4 0.9 %copy-done.5 = bf16[128,1024]{1,0:T(8,128)(2,1)S(1)} copy-done((bf16[128,1024]{1,0:T(8,128)(2,1)S(1)}, bf16[128,1024]{1,0:T(8,128)(2,1)}, u32[]{:S(2)}) %copy-start.5) | copy-done | bytes 262168
  6.3 0.0 copy-start.6
  6.3 0.8 %copy-done.6 = bf16[128,128]{1,0:T(8,128)(2,1)S(1)} copy-done((bf16[128,128]{1,0:T(8,128)(2,1)S(1)}, bf16[128,128]{1,0:T(8,128)(2,1)}, u32[]{:S(2)}) %copy-start.6) | copy-done | bytes 32792
  7.1 0.0 copy-start.7
  7.1 0.8 %copy-done.7 = bf16[128,128]{1,0:T(8,128)(2,1)S(1)} copy-done((bf16[128,128]{1,0:T(8,128)(2,1)S(1)}, bf16[128,128]{1,0:T(8,128)(2,1)}, u32[]{:S(2)}) %copy-start.7) | copy-done | bytes 32792
  7.9 0.0 copy-start.8
  7.9 0.7 copy-done.8
  8.5 0.0 copy-start.9
  8.5 0.7 copy-done.9
  9.2 63.3 %grads.1 = (f32[128,1024]{1,0:T(8,128)S(1)}, f32[128,1024]{1,0:T(8,128)S(1)}, f32[128,1024]{1,0:T(8,128)S(1)}, f32[8,128]{1,0:T(8,128)S(1)}, f32[128,1024]{1,0:T...) custom-call(bf16[128,1024]{1,0:T(8,128)(2,1)S(1)} %copy-done, bf16[128,1024]{1,0:T(8,128)(2,1)S(1)} %copy-done.1, ...), custom_call_target="tpu_custom_call" | custom-call | tf_op jit(solution)/shard_map/grads/pallas_call | solution.py:524
  72.5 1.4 %finish.1 = (f32[128,1024]{1,0:T(8,128)}, f32[128,1024]{1,0:T(8,128)}, f32[128,1024]{1,0:T(8,128)}, f32[8,128]{1,0:T(8,128)}, f32[128,1024]{1,0:T(8,128)}, /*index=5*/f32[128,128]{1,0:T(8,128)}, f32[128,128]{1,0:T(8,128)}) custom-call(f32[128,1024]{1,0:T(8,128)S(1)} %get-tuple-element.21.refs_0_, f32[128,1024]{1,0:T(8,128)S(1)} %get-tuple-element.22.refs_1_, ...), custom_call_target="tpu_custom_call" | custom-call | tf_op jit(solution)/shard_map/finish/pallas_call | solution.py:535
Async XLA Ops:
  0.6 1.0 %copy-start = (bf16[128,1024]{1,0:T(8,128)(2,1)S(1)}, bf16[128,1024]{1,0:T(8,128)(2,1)}, u32[]{:S(2)}) copy-start(bf16[128,1024]{1,0:T(8,128)(2,1)} %lq.1) | copy-start | bytes 786436
  1.6 0.9 %copy-start.1 = (bf16[128,1024]{1,0:T(8,128)(2,1)S(1)}, bf16[128,1024]{1,0:T(8,128)(2,1)}, u32[]{:S(2)}) copy-start(bf16[128,1024]{1,0:T(8,128)(2,1)} %lk.1) | copy-start | bytes 786436
  2.5 0.9 %copy-start.2 = (bf16[128,1024]{1,0:T(8,128)(2,1)S(1)}, bf16[128,1024]{1,0:T(8,128)(2,1)}, u32[]{:S(2)}) copy-start(bf16[128,1024]{1,0:T(8,128)(2,1)} %lv.1) | copy-start | bytes 786436
  3.5 0.9 %copy-start.3 = (bf16[128,1024]{1,0:T(8,128)(2,1)S(1)}, bf16[128,1024]{1,0:T(8,128)(2,1)}, u32[]{:S(2)}) copy-start(bf16[128,1024]{1,0:T(8,128)(2,1)} %lc.1) | copy-start | bytes 786436
  4.4 0.9 %copy-start.4 = (bf16[128,1024]{1,0:T(8,128)(2,1)S(1)}, bf16[128,1024]{1,0:T(8,128)(2,1)}, u32[]{:S(2)}) copy-start(bf16[128,1024]{1,0:T(8,128)(2,1)} %sq.1) | copy-start | bytes 786436
  5.4 0.9 %copy-start.5 = (bf16[128,1024]{1,0:T(8,128)(2,1)S(1)}, bf16[128,1024]{1,0:T(8,128)(2,1)}, u32[]{:S(2)}) copy-start(bf16[128,1024]{1,0:T(8,128)(2,1)} %sc.1) | copy-start | bytes 786436
  6.3 0.8 %copy-start.6 = (bf16[128,128]{1,0:T(8,128)(2,1)S(1)}, bf16[128,128]{1,0:T(8,128)(2,1)}, u32[]{:S(2)}) copy-start(bf16[128,128]{1,0:T(8,128)(2,1)} %sk.1) | copy-start | bytes 98308
  7.1 0.8 %copy-start.7 = (bf16[128,128]{1,0:T(8,128)(2,1)S(1)}, bf16[128,128]{1,0:T(8,128)(2,1)}, u32[]{:S(2)}) copy-start(bf16[128,128]{1,0:T(8,128)(2,1)} %sv.1) | copy-start | bytes 98308
  7.9 0.7 copy-start.8
  8.5 0.7 copy-start.9

commit v3 on v2

--- a/solution.py
+++ b/solution.py
@@ -36,12 +36,12 @@
 
 def kernel(
     n, nh, gy,
-    lq, lk, lv, ld, gain, lc, sq, sk, sv, sc,
+    lq_h, lk_h, lv_h, ld_h, gain_h, lc_h, sq_h, sk_h, sv_h, sc_h,
     o_dq, o_dk, o_dv, o_gg, o_sdq, o_sdk, o_sdv,
     sbuf, dpbuf, kv, pbuf, prec, osend, orec, xsend, xrec, acc,
     qt, ct, qr, cr, dscb, pb, dqt, m8, l8, d8,
     ms, pw, out, dout, lsend, lrec, esend, erec, wsend, wrec, asend, arec,
-    dec, decs, ggs, ggr, pss, psr,
+    dec, decs, ggs, ggr, pss, psr, lq, lk, lv, ld, gain, lc, sq, sc, in_s,
     a2a_s, a2a_r, kv_s, kv_f, kv_r, pr_s, pr_r, os_s, os_r, xs_s, xs_r,
 ):
     me = lax.axis_index("ctx")
@@ -56,6 +56,26 @@
     rs = D // spn
     width = H * D
 
+    loads = [
+        pltpu.make_async_copy(a, b, in_s.at[i])
+        for i, (a, b) in enumerate(
+            [
+                (ld_h, ld),
+                (lk_h, lk),
+                (lv_h, lv),
+                (sk_h, kv.at[chip, core, 0]),
+                (sv_h, kv.at[chip, core, 1]),
+                (lq_h, lq),
+                (sq_h, sq),
+                (sc_h, sc),
+                (lc_h, lc),
+                (gain_h, gain),
+            ]
+        )
+    ]
+    for load in loads:
+        load.start()
+
     barrier = pltpu.get_barrier_semaphore()
 
     @pl.loop(1, n)
@@ -70,13 +90,11 @@
             barrier, inc=1, device_id={"head": lax.rem(hd + d, nh)}, device_id_type=MESH
         )
 
-    kv[chip, core, 0] = sk[...]
-    kv[chip, core, 1] = sv[...]
-
     row_i = lax.broadcasted_iota(jnp.int32, (D, D), 0)
     col_i = lax.broadcasted_iota(jnp.int32, (D, D), 1)
     causal = col_i <= row_i
     tri = jnp.where(causal, 1.0, 0.0).astype(F32)
+    loads[0].wait()
     ldv = ld[...]
     cum = dot(tri, ldv, 1, 1, HIGH)
     cum_t = dot(ldv, tri, 1, 1, HIGH)
@@ -87,6 +105,8 @@
     def col(a, h):
         return jnp.broadcast_to(a[:, h : h + 1], (D, D))
 
+    loads[1].wait()
+    loads[2].wait()
     for h in range(H):
         kd = (lk[:, hs(h)].astype(F32) * col(kdec, h)).astype(BF16)
         local = dot(kd, lv[:, hs(h)], 0, 0)
@@ -95,6 +115,8 @@
     lrec[me] = lsend[me]
     decs[me] = dec[me // spn]
 
+    for load in loads[3:]:
+        load.wait()
     pl.semaphore_wait(barrier, n - 1 + nh - 1)
 
     def exchange(src, dst, k, by_target=True, pick=None):
@@ -318,13 +340,6 @@
         qr[h * D : (h + 1) * D, :] = (sq[:, hs(h)].astype(F32) * (rc * SCALE)).astype(BF16)
         cr[h * D : (h + 1) * D, :] = (sc[:, hs(h)].astype(F32) * rc).astype(BF16)
 
-    arrived(arec, 6, n - 1)
-    for h in range(H):
-        a = state(arec, h)
-        kd = SCALE * col(kdec, h)
-        o_dk[:, hs(h)] += kd * dot(lv[:, hs(h)], a, 1, 1)
-        o_dv[:, hs(h)] += kd * dot(lk[:, hs(h)], a)
-
     dqt[...] = jnp.zeros((D, width), F32)
 
     def pair_copy(k):
@@ -385,6 +400,13 @@
         @pl.when(k > 0)
         def _():
             own_send(k - 1)
+
+    arrived(arec, 6, n - 1)
+    for h in range(H):
+        a = state(arec, h)
+        kd = SCALE * col(kdec, h)
+        o_dk[:, hs(h)] += kd * dot(lv[:, hs(h)], a, 1, 1)
+        o_dv[:, hs(h)] += kd * dot(lk[:, hs(h)], a)
 
     for h in range(H):
         o_sdq[:, hs(h)] = (dqt[:, hs(h)] * (rinv[:, hs(h)] * SCALE)).T
@@ -506,6 +528,15 @@
         pltpu.VMEM((n, H, D), F32),
         pltpu.VMEM((2, 8, D), F32),
         pltpu.VMEM((nh, 2, 8, D), F32),
+        pltpu.VMEM((D, width), BF16),
+        pltpu.VMEM((D, width), BF16),
+        pltpu.VMEM((D, width), BF16),
+        pltpu.VMEM((H, D), F32),
+        pltpu.VMEM((1, width), F32),
+        pltpu.VMEM((D, width), BF16),
+        pltpu.VMEM((D, width), BF16),
+        pltpu.VMEM((D, width), BF16),
+        pltpu.SemaphoreType.DMA((10,)),
         pltpu.SemaphoreType.DMA((7,)),
         pltpu.SemaphoreType.DMA((7,)),
         pltpu.SemaphoreType.DMA((nc,)),
@@ -518,17 +549,17 @@
         pltpu.SemaphoreType.DMA((gx,)),
         pltpu.SemaphoreType.DMA((gx,)),
     ]
-    big = jax.ShapeDtypeStruct((D, width), F32)
-    small = jax.ShapeDtypeStruct((D, D), F32)
+    big = pltpu.VMEM((D, width), F32)
+    small = pltpu.VMEM((D, D), F32)
     vmem = pl.BlockSpec(memory_space=pltpu.VMEM)
     res = pl.pallas_call(
         functools.partial(kernel, n, nh, gy),
-        out_shape=(big, big, big, jax.ShapeDtypeStruct((H, D), F32), big, small, small),
-        in_specs=[vmem] * 10,
+        out_shape=(big, big, big, pltpu.VMEM((H, D), F32), big, small, small),
+        in_specs=[pl.BlockSpec(memory_space=pltpu.HBM)] * 10,
         out_specs=(vmem,) * 7,
         scratch_shapes=scratch,
         compiler_params=pltpu.CompilerParams(
-            collective_id=0, has_side_effects=True, vmem_limit_bytes=48 * 1024 * 1024
+            collective_id=0, has_side_effects=True, vmem_limit_bytes=56 * 1024 * 1024
         ),
         name="grads",
     )(lq, lk, lv, ld.T, gain.reshape(1, width), lc, sq, sk, sv, sc)

time: 74.7 us -> 65.2 us (0.87)
  local copies, waits for them, and re-layouts: 8.58 us -> 0 us
    unnamed x20 -> x0, local copies, waits for them, and re-layouts: 8.58 us -> none
where the time goes in v3:
time: 65.2 us; the launch traced here: 64.8 us
  Pallas kernels  64.1 us (98%)
    pallas_call x1, Pallas kernels, on_device(): pl.pallas_call(functools.partial(kernel, n, nh, gy), out_shape=(big, big,...  62.7 us
    pallas_call x1, Pallas kernels, on_device(): pl.pallas_call(finish, out_shape=tuple((jax.ShapeDtypeStruct(r.shape, r.d...  1.41 us

profile of v3, /device:TPU:26, one launch (start us, length us, event | category | flops | bytes accessed | tf_op | source)
XLA Modules:
  0.0 64.8 jit_solution(1367338238224364253)
XLA Ops:
  0.6 62.7 %grads.1 = (f32[128,1024]{1,0:T(8,128)S(1)}, f32[128,1024]{1,0:T(8,128)S(1)}, f32[128,1024]{1,0:T(8,128)S(1)}, f32[8,128]{1,0:T(8,128)S(1)}, f32[128,1024]{1,0:T...) custom-call(bf16[128,1024]{1,0:T(8,128)(2,1)} %lq_h.1, bf16[128,1024]{1,0:T(8,128)(2,1)} %lk_h.1, ...), custom_call_target="tpu_custom_call" | custom-call | tf_op jit(solution)/shard_map/grads/pallas_call | solution.py:555
  63.4 1.4 %finish.1 = (f32[128,1024]{1,0:T(8,128)}, f32[128,1024]{1,0:T(8,128)}, f32[128,1024]{1,0:T(8,128)}, f32[8,128]{1,0:T(8,128)}, f32[128,1024]{1,0:T(8,128)}, /*index=5*/f32[128,128]{1,0:T(8,128)}, f32[128,128]{1,0:T(8,128)}) custom-call(f32[128,1024]{1,0:T(8,128)S(1)} %get-tuple-element.21.refs_0_, f32[128,1024]{1,0:T(8,128)S(1)} %get-tuple-element.22.refs_1_, ...), custom_call_target="tpu_custom_call" | custom-call | tf_op jit(solution)/shard_map/finish/pallas_call | solution.py:566

commit v4 on v3

--- a/solution.py
+++ b/solution.py
@@ -42,7 +42,7 @@
     qt, ct, qr, cr, dscb, pb, dqt, m8, l8, d8,
     ms, pw, out, dout, lsend, lrec, esend, erec, wsend, wrec, asend, arec,
     dec, decs, ggs, ggr, pss, psr, lq, lk, lv, ld, gain, lc, sq, sc, in_s,
-    a2a_s, a2a_r, kv_s, kv_f, kv_r, pr_s, pr_r, os_s, os_r, xs_s, xs_r,
+    a2a_s, a2a_r, h_s, h_r, kv_s, kv_f, kv_r, pr_s, pr_r, os_s, os_r, xs_s, xs_r,
 ):
     me = lax.axis_index("ctx")
     hd = lax.axis_index("head")
@@ -144,8 +144,37 @@
         part = dst.at[pl.ds(0, count)]
         pltpu.make_async_copy(part, part, a2a_s.at[k]).wait()
 
-    exchange(lsend, lrec, 0)
+    half = rs // 2
+
+    def exchange_half(src, dst, k, i):
+        rows = pl.ds(i * half, half)
+
+        @pl.loop(1, n)
+        def _(d):
+            to = lax.rem(me + d, n)
+            pltpu.make_async_remote_copy(
+                src_ref=src.at[to, rows],
+                dst_ref=dst.at[me, rows],
+                send_sem=h_s.at[k, i],
+                recv_sem=h_r.at[k, i],
+                device_id={"ctx": to},
+                device_id_type=MESH,
+            ).start()
+
+    def half_wait(ref, sem, k, i):
+        part = ref.at[pl.ds(0, n - 1), pl.ds(i * half, half)]
+        pltpu.make_async_copy(part, part, sem.at[k, i]).wait()
+
+    def scan(src, dst, i, order):
+        rows = slice(i * half, (i + 1) * half)
+        run = jnp.zeros((half, D), F32)
+        for c in order:
+            dst[c, rows] = run.astype(BF16)
+            run = jnp.broadcast_to(decs[c], (half, D)) * run + src[c, rows].astype(F32)
+
     exchange(dec, decs, 1, pick=lambda to: to // spn)
+    exchange_half(lsend, lrec, 0, 0)
+    exchange_half(lsend, lrec, 0, 1)
 
     def kv_copy(k, sem, to):
         return pltpu.make_async_remote_copy(
@@ -215,14 +244,12 @@
         qt[:, hs(h)] = qh.T
         ct[:, hs(h)] = chh.T
 
-    arrived(lrec, 0, n - 1)
     arrived(decs, 1, n - 1)
-    run = jnp.zeros((rs, D), F32)
-    for c in range(n):
-        esend[c] = run.astype(BF16)
-        run = jnp.broadcast_to(decs[c], (rs, D)) * run + lrec[c].astype(F32)
+    for i in range(2):
+        half_wait(lrec, h_r, 0, i)
+        scan(lrec, esend, i, range(n))
+        exchange_half(esend, erec, 1, i)
     erec[me] = esend[me]
-    exchange(esend, erec, 2)
     kv_spread()
 
     def scores(k, masked):
@@ -242,7 +269,8 @@
     kv_wait(chip, 1 - core)
     scores(chip, True)
 
-    arrived(erec, 2, n - 1)
+    half_wait(erec, h_r, 1, 0)
+    half_wait(erec, h_r, 1, 1)
 
     def state(ref, h):
         return ref[h * spn : (h + 1) * spn].reshape(D, D)
@@ -295,7 +323,8 @@
         wsend[h * spn : (h + 1) * spn] = dot(qd, do, 0, 0).astype(BF16).reshape(spn, rs, D)
     wrec[me] = wsend[me]
     ggr[me] = ggs[...]
-    exchange(wsend, wrec, 4)
+    exchange_half(wsend, wrec, 2, 0)
+    exchange_half(wsend, wrec, 2, 1)
     exchange(ggs, ggr, 5, by_target=False)
 
     for h in range(H):
@@ -305,19 +334,17 @@
         o_dk[:, hs(h)] = dot(dp, lq[:, hs(h)], 0, 0)
         o_dv[:, hs(h)] = dot(pw[h], do, 0, 0)
 
-    arrived(wrec, 4, n - 1)
-    run = jnp.zeros((rs, D), F32)
-    for c in range(n - 1, -1, -1):
-        asend[c] = run.astype(BF16)
-        run = jnp.broadcast_to(decs[c], (rs, D)) * run + wrec[c].astype(F32)
-    arec[me] = asend[me]
-    exchange(asend, arec, 6)
-
     @pl.loop(chip // 2, chip)
     def _(i):
         k = chip - 1 - i
         kv_wait(k, 1 - core)
         scores(k, False)
+
+    for i in range(2):
+        half_wait(wrec, h_r, 2, i)
+        scan(wrec, asend, i, range(n - 1, -1, -1))
+        exchange_half(asend, arec, 3, i)
+    arec[me] = asend[me]
 
     factor = SCALE * LOG2E
     top = jnp.max(m8[...], axis=0, keepdims=True) * factor
@@ -401,7 +428,8 @@
         def _():
             own_send(k - 1)
 
-    arrived(arec, 6, n - 1)
+    half_wait(arec, h_r, 3, 0)
+    half_wait(arec, h_r, 3, 1)
     for h in range(H):
         a = state(arec, h)
         kd = SCALE * col(kdec, h)
@@ -444,13 +472,12 @@
     o_sdk[...] = acc[0]
     o_sdv[...] = acc[1]
 
-    left(lsend, 0, n - 1)
+    for k, ref in enumerate((lsend, esend, wsend, asend)):
+        half_wait(ref, h_s, k, 0)
+        half_wait(ref, h_s, k, 1)
     left(decs, 1, n - 1)
-    left(esend, 2, n - 1)
     left(psr, 3, nh - 1)
-    left(wsend, 4, n - 1)
     left(ggr, 5, n - 1)
-    left(asend, 6, n - 1)
 
     @pl.loop(0, nc)
     def _(k):
@@ -539,6 +566,8 @@
         pltpu.SemaphoreType.DMA((10,)),
         pltpu.SemaphoreType.DMA((7,)),
         pltpu.SemaphoreType.DMA((7,)),
+        pltpu.SemaphoreType.DMA((4, 2)),
+        pltpu.SemaphoreType.DMA((4, 2)),
         pltpu.SemaphoreType.DMA((nc,)),
         pltpu.SemaphoreType.DMA((nc,)),
         pltpu.SemaphoreType.DMA((nc, 2)),

time: 65.2 us -> 64.8 us (level)
  no operation moved by 1% of the time
where the time goes in v4:
time: 64.8 us; the launch traced here: 64.7 us
  Pallas kernels  64 us (99%)
    pallas_call x1, Pallas kernels, on_device(): pl.pallas_call(functools.partial(kernel, n, nh, gy), out_shape=(big, big,...  62.6 us
    pallas_call x1, Pallas kernels, on_device(): pl.pallas_call(finish, out_shape=tuple((jax.ShapeDtypeStruct(r.shape, r.d...  1.41 us

profile of v4, /device:TPU:26, one launch (start us, length us, event | category | flops | bytes accessed | tf_op | source)
XLA Modules:
  0.0 64.7 jit_solution(4596451771141391599)
XLA Ops:
  0.6 62.6 %grads.1 = (f32[128,1024]{1,0:T(8,128)S(1)}, f32[128,1024]{1,0:T(8,128)S(1)}, f32[128,1024]{1,0:T(8,128)S(1)}, f32[8,128]{1,0:T(8,128)S(1)}, f32[128,1024]{1,0:T...) custom-call(bf16[128,1024]{1,0:T(8,128)(2,1)} %lq_h.1, bf16[128,1024]{1,0:T(8,128)(2,1)} %lk_h.1, ...), custom_call_target="tpu_custom_call" | custom-call | tf_op jit(solution)/shard_map/grads/pallas_call | solution.py:584
  63.2 1.4 %finish.1 = (f32[128,1024]{1,0:T(8,128)}, f32[128,1024]{1,0:T(8,128)}, f32[128,1024]{1,0:T(8,128)}, f32[8,128]{1,0:T(8,128)}, f32[128,1024]{1,0:T(8,128)}, /*index=5*/f32[128,128]{1,0:T(8,128)}, f32[128,128]{1,0:T(8,128)}) custom-call(f32[128,1024]{1,0:T(8,128)S(1)} %get-tuple-element.21.refs_0_, f32[128,1024]{1,0:T(8,128)S(1)} %get-tuple-element.22.refs_1_, ...), custom_call_target="tpu_custom_call" | custom-call | tf_op jit(solution)/shard_map/finish/pallas_call | solution.py:595

commit v5 on v4

--- a/solution.py
+++ b/solution.py
@@ -299,14 +299,6 @@
             device_id_type=MESH,
         ).start()
 
-    kv_relay()
-
-    @pl.loop(0, chip // 2)
-    def _(i):
-        k = chip - 1 - i
-        kv_wait(k, 1 - core)
-        scores(k, False)
-
     arrived(psr, 3, nh - 1)
     sums = jnp.sum(psr[...], axis=0)
     inv = lax.rsqrt(sums[0, 0:1] / (nh * width) + EPS)
@@ -334,7 +326,9 @@
         o_dk[:, hs(h)] = dot(dp, lq[:, hs(h)], 0, 0)
         o_dv[:, hs(h)] = dot(pw[h], do, 0, 0)
 
-    @pl.loop(chip // 2, chip)
+    kv_relay()
+
+    @pl.loop(0, chip)
     def _(i):
         k = chip - 1 - i
         kv_wait(k, 1 - core)

time: 64.8 us -> 64.6 us (level); the launches traced: 64.7 us -> 63.7 us
  Pallas kernels: 64 us -> 63.1 us
    pallas_call x1, Pallas kernels: 62.6 us -> 61.7 us  [on_device(): pl.pallas_call(functools.partial(kernel, n, nh, gy), out_shape=(big, big,...]
where the time goes in v5:
time: 64.6 us; the launch traced here: 63.7 us
  Pallas kernels  63.1 us (98%)
    pallas_call x1, Pallas kernels, on_device(): pl.pallas_call(functools.partial(kernel, n, nh, gy), out_shape=(big, big,...  61.7 us
    pallas_call x1, Pallas kernels, on_device(): pl.pallas_call(finish, out_shape=tuple((jax.ShapeDtypeStruct(r.shape, r.d...  1.41 us

profile of v5, /device:TPU:26, one launch (start us, length us, event | category | flops | bytes accessed | tf_op | source)
XLA Modules:
  0.0 63.7 jit_solution(11072051217193691301)
XLA Ops:
  0.6 61.7 %grads.1 = (f32[128,1024]{1,0:T(8,128)S(1)}, f32[128,1024]{1,0:T(8,128)S(1)}, f32[128,1024]{1,0:T(8,128)S(1)}, f32[8,128]{1,0:T(8,128)S(1)}, f32[128,1024]{1,0:T...) custom-call(bf16[128,1024]{1,0:T(8,128)(2,1)} %lq_h.1, bf16[128,1024]{1,0:T(8,128)(2,1)} %lk_h.1, ...), custom_call_target="tpu_custom_call" | custom-call | tf_op jit(solution)/shard_map/grads/pallas_call | solution.py:578
  62.3 1.4 %finish.1 = (f32[128,1024]{1,0:T(8,128)}, f32[128,1024]{1,0:T(8,128)}, f32[128,1024]{1,0:T(8,128)}, f32[8,128]{1,0:T(8,128)}, f32[128,1024]{1,0:T(8,128)}, /*index=5*/f32[128,128]{1,0:T(8,128)}, f32[128,128]{1,0:T(8,128)}) custom-call(f32[128,1024]{1,0:T(8,128)S(1)} %get-tuple-element.21.refs_0_, f32[128,1024]{1,0:T(8,128)S(1)} %get-tuple-element.22.refs_1_, ...), custom_call_target="tpu_custom_call" | custom-call | tf_op jit(solution)/shard_map/finish/pallas_call | solution.py:589
